TPU v7x, 256 devices: a whole 4x4x8 slice. The times are simulated.
256 devices in a mesh: seg: 16 (over x, y_hi, core), gx: 16 (over z, y_lo).
Axes of the slice: x: 4, y: 4 (y_hi: 2, y_lo: 2; y = y_hi * 2 + y_lo), z: 8, core: 2. Of those that a mesh axis runs over, the one named last changes fastest.
Arguments:
- adjoint_in: float32 [16, 5, 256, 32, 512], P('seg', None, 'gx'), may hold values from -6 to 6
- sensor: float32 [16, 256, 32, 512], P('seg', 'gx'), may hold values from 0.06 to 0.15
- filter_matrix: float32 [512, 512], replicated
- coupling: float32 [5, 5], replicated
Outputs:
- adjoint_out: float32 [16, 5, 256, 32, 512], P('seg', None, 'gx')
All inputs are finite; a program needn't handle non-finite values.
Results may differ from a plain program's by a relative error of at most 0.00017.
Values sent between devices are 32-bit elements; how exact they have to be, the bound alone decides.
A program may use at most 64 MiB of HBM per device.

v0:
```python
import functools

import jax
import jax.numpy as jnp
from jax import lax
from jax.experimental import pallas as pl
from jax.experimental.pallas import tpu as pltpu
from jax.sharding import PartitionSpec as P

STEPS = 3
FIRST = 2
MESH = pl.DeviceIdType.MESH


def kernel(a_ref, s_ref, w_ref, c_ref, out_ref, planes, own, sens, wide, wcat, xcat, filt, mixd, ssem, rsem, lsem, gsem):
    fields, cx, nt, nr = out_ref.shape
    total = cx + 2 * STEPS
    half = nt // 2
    seg, gx = lax.axis_index("seg"), lax.axis_index("gx")
    nseg, ngx = lax.axis_size("seg"), lax.axis_size("gx")
    after, before = lax.rem(seg + 1, nseg), lax.rem(seg + nseg - 1, nseg)
    has_low, has_high = gx > 0, gx < ngx - 1
    low, high = jnp.maximum(gx - 1, 0), jnp.minimum(gx + 1, ngx - 1)
    lows, highs = has_low.astype(jnp.int32), has_high.astype(jnp.int32)
    leaves = lax.rem(seg, 2) == 0
    crosses = jnp.logical_and(leaves, lax.rem(lax.div(seg, 2), 2) == 0)
    held = jnp.where(crosses, lax.rem(seg + nseg - 4, nseg), seg)
    freed = jnp.where(crosses, lax.rem(seg + 4, nseg), seg)

    barrier = pltpu.get_barrier_semaphore()

    def greet(device):
        pl.semaphore_signal(barrier, inc=1, device_id=device, device_id_type=MESH)

    greet((after, gx))

    @pl.when(has_low)
    def _():
        greet((after, low))
        greet((seg, low))

    @pl.when(has_high)
    def _():
        greet((after, high))
        greet((seg, high))

    @pl.when(jnp.logical_and(crosses, has_low))
    def _():
        greet((held, low))

    @pl.when(jnp.logical_and(crosses, has_high))
    def _():
        greet((held, high))

    def own_copy(i):
        return pltpu.make_async_copy(a_ref.at[0, :, i], own.at[i], lsem.at[2 + i])

    w_copy = pltpu.make_async_copy(w_ref, wide, lsem.at[0])
    s_copy = pltpu.make_async_copy(s_ref.at[0], sens.at[pl.ds(2, cx)], lsem.at[1])
    w_copy.start()
    s_copy.start()
    for j in range(cx):
        own_copy(j).start()

    def plane_copy(source, slot, sem, device):
        return pltpu.make_async_remote_copy(
            src_ref=a_ref.at[0, :, source],
            dst_ref=planes.at[slot],
            send_sem=ssem.at[sem],
            recv_sem=rsem.at[slot],
            device_id=device,
            device_id_type=MESH,
        )

    def sens_copy(source, slot, sem, device):
        return pltpu.make_async_remote_copy(
            src_ref=s_ref.at[0, pl.ds(source, 2)],
            dst_ref=sens.at[pl.ds(slot, 2)],
            send_sem=ssem.at[total + sem],
            recv_sem=rsem.at[total + sem],
            device_id=device,
            device_id_type=MESH,
        )

    def to_high(j):
        return plane_copy(cx - STEPS + j, j, j, (before, high))

    def to_same(j):
        return plane_copy(j, STEPS + j, STEPS + j, (before, gx))

    def to_low(j):
        return plane_copy(j, STEPS + cx + j, STEPS + cx + j, (before, low))

    sens_to_high = sens_copy(cx - 2, 0, 0, (seg, high))
    sens_to_low = sens_copy(0, cx + 2, 1, (seg, low))

    pl.semaphore_wait(barrier, 1 + (2 + crosses.astype(jnp.int32)) * (lows + highs))

    @pl.when(has_high)
    def _():
        sens_to_high.start()

    @pl.when(has_low)
    def _():
        sens_to_low.start()

    for j in range(STEPS):

        @pl.when(has_high)
        def _():
            to_high(j).start()

        @pl.when(has_low)
        def _():
            to_low(j).start()

    for j in range(FIRST):
        to_same(j).start()

    @pl.when(jnp.logical_not(leaves))
    def _():
        for j in range(FIRST, cx):
            to_same(j).start()

    @pl.when(jnp.logical_not(has_low))
    def _():
        sens[pl.ds(0, 2)] = jnp.zeros((2, nt, nr), jnp.float32)
        planes[pl.ds(0, STEPS)] = jnp.zeros((STEPS, fields, nt, nr), jnp.float32)

    @pl.when(jnp.logical_not(has_high))
    def _():
        sens[pl.ds(cx + 2, 2)] = jnp.zeros((2, nt, nr), jnp.float32)
        planes[pl.ds(cx + STEPS, STEPS)] = jnp.zeros((STEPS, fields, nt, nr), jnp.float32)

    for step in range(STEPS):
        for slot in range(3):
            for f in range(fields):
                mixd[step, slot, f, pl.ds(0, 8)] = jnp.zeros((8, nr), jnp.float32)
                mixd[step, slot, f, pl.ds(8 + nt, 8)] = jnp.zeros((8, nr), jnp.float32)

    w_copy.wait()
    block = 64
    for i in range(nr // block):
        w = wide[pl.ds(i * block, block)]
        w_hi = w.astype(jnp.bfloat16)
        w_lo = (w - w_hi.astype(jnp.float32)).astype(jnp.bfloat16)
        wcat[pl.ds(i * block, block)] = w_hi
        wcat[pl.ds(nr + i * block, block)] = w_hi
        wcat[pl.ds(2 * nr + i * block, block)] = w_lo
    s_copy.wait()

    @pl.when(has_low)
    def _():
        sens_copy(cx - 2, 0, 0, (seg, high)).wait_recv()

    @pl.when(has_high)
    def _():
        sens_copy(0, cx + 2, 1, (seg, low)).wait_recv()

    def arrival(i):
        plane_copy(0, i, i, (before, gx)).wait_recv()

    @pl.when(jnp.logical_and(leaves, has_low))
    def _():
        for j in range(STEPS):
            arrival(j)
        pl.semaphore_signal(gsem, inc=1, device_id=(freed, low), device_id_type=MESH)

    @pl.when(jnp.logical_and(leaves, has_high))
    def _():
        for j in range(STEPS):
            arrival(STEPS + cx + j)
        pl.semaphore_signal(gsem, inc=1, device_id=(freed, high), device_id_type=MESH)

    @pl.when(leaves)
    def _():
        pl.semaphore_wait(gsem, lows + highs)
        for j in range(FIRST, cx):
            to_same(j).start()

    lane = lax.broadcasted_iota(jnp.int32, (half, nr), 1)

    def put(f, h, x):
        rows = pl.ds(f * nt + h * half, half)
        x_hi = x.astype(jnp.bfloat16)
        x_lo = (x - x_hi.astype(jnp.float32)).astype(jnp.bfloat16)
        xcat[rows, pl.ds(0, nr)] = x_hi
        xcat[rows, pl.ds(nr, nr)] = x_lo
        xcat[rows, pl.ds(2 * nr, nr)] = x_hi

    def filter_and_mix(step, i):
        two, three = lax.rem(i, 2), lax.rem(i, 3)
        filt[step, two] = jnp.dot(xcat[...], wcat[...], preferred_element_type=jnp.float32).reshape(fields, nt, nr)
        for t in range(nt // 8):
            rows = pl.ds(t * 8, 8)
            v = [filt[step, two, g, rows] for g in range(fields)]
            for f in range(fields):
                m = c_ref[0, f] * v[0]
                for g in range(1, fields):
                    m = m + c_ref[g, f] * v[g]
                mixd[step, three, f, pl.ds(8 + t * 8, 8)] = m

    def stencil(step, i, use):
        two = lax.rem(i, 2)
        mid, lo, hi = lax.rem(i, 3), lax.rem(i + 2, 3), lax.rem(i + 1, 3)
        for h in range(2):
            s = sens[i - 1, pl.ds(h * half, half)]
            for f in range(fields):
                at = 8 + h * half
                m = mixd[step, mid, f, pl.ds(at, half)]
                total_ = mixd[step, lo, f, pl.ds(at, half)] + mixd[step, hi, f, pl.ds(at, half)]
                total_ = total_ + mixd[step, mid, f, pl.ds(at - 1, half)] + mixd[step, mid, f, pl.ds(at + 1, half)]
                left = jnp.where(lane == 0, 0.0, pltpu.roll(m, 1, 1))
                right = jnp.where(lane == nr - 1, 0.0, pltpu.roll(m, nr - 1, 1))
                total_ = total_ + left + right - 6.0 * m
                use(f, h, filt[step, two, f, pl.ds(h * half, half)] + s * total_)

    def arrive(i, carry):
        slab = jnp.logical_and(i >= STEPS, i < STEPS + cx)
        halo = jnp.logical_or(jnp.logical_and(i < STEPS, has_low), jnp.logical_and(i >= STEPS + cx, has_high))

        @pl.when(jnp.logical_or(slab, jnp.logical_and(halo, jnp.logical_not(leaves))))
        def _():
            arrival(i)

        for h in range(2):
            for f in range(fields):
                put(f, h, planes[i, f, pl.ds(h * half, half)])
        filter_and_mix(0, i)

        @pl.when(i >= 2)
        def _():
            stencil(0, i - 1, put)
            filter_and_mix(1, i - 1)

        @pl.when(i >= 4)
        def _():
            stencil(1, i - 2, put)
            filter_and_mix(2, i - 2)

        @pl.when(i >= 6)
        def _():
            o = i - 2 * STEPS
            pltpu.make_async_copy(a_ref.at[0, :, o], own.at[o], lsem.at[2 + o]).wait()

            def write(f, h, x):
                rows = pl.ds(h * half, half)
                out_ref[f, o, rows] = x - own[o, f, rows]

            stencil(2, i - 3, write)

        return carry

    lax.fori_loop(0, total, arrive, 0)

    @pl.when(has_high)
    def _():
        sens_to_high.wait_send()
        for j in range(STEPS):
            to_high(j).wait_send()

    for j in range(cx):
        to_same(j).wait_send()

    @pl.when(has_low)
    def _():
        sens_to_low.wait_send()
        for j in range(STEPS):
            to_low(j).wait_send()


def shards(adjoint_in, sensor, filter_matrix, coupling):
    _, fields, cx, nt, nr = adjoint_in.shape
    total = cx + 2 * STEPS
    out = pl.pallas_call(
        kernel,
        out_shape=pltpu.VMEM((fields, cx, nt, nr), jnp.float32),
        in_specs=[
            pl.BlockSpec(memory_space=pltpu.HBM),
            pl.BlockSpec(memory_space=pltpu.HBM),
            pl.BlockSpec(memory_space=pltpu.HBM),
            pl.BlockSpec(memory_space=pltpu.SMEM),
        ],
        out_specs=pl.BlockSpec(memory_space=pltpu.VMEM),
        scratch_shapes=[
            pltpu.VMEM((total, fields, nt, nr), jnp.float32),
            pltpu.VMEM((cx, fields, nt, nr), jnp.float32),
            pltpu.VMEM((cx + 4, nt, nr), jnp.float32),
            pltpu.VMEM((nr, nr), jnp.float32),
            pltpu.VMEM((3 * nr, nr), jnp.bfloat16),
            pltpu.VMEM((fields * nt, 3 * nr), jnp.bfloat16),
            pltpu.VMEM((STEPS, 2, fields, nt, nr), jnp.float32),
            pltpu.VMEM((STEPS, 3, fields, nt + 16, nr), jnp.float32),
            pltpu.SemaphoreType.DMA((total + 2,)),
            pltpu.SemaphoreType.DMA((total + 2,)),
            pltpu.SemaphoreType.DMA((cx + 2,)),
            pltpu.SemaphoreType.REGULAR,
        ],
        compiler_params=pltpu.CompilerParams(collective_id=0, has_side_effects=True, vmem_limit_bytes=61_400_000),
        name="shooting",
    )(adjoint_in, sensor, filter_matrix, coupling)
    return out[None]


def solution(mesh):
    in_specs = (P("seg", None, "gx", None, None), P("seg", "gx", None, None), P(), P())
    out_specs = P("seg", None, "gx", None, None)
    return jax.shard_map(shards, mesh=mesh, in_specs=in_specs, out_specs=out_specs, check_vma=False)
```

profile of v0, /device:TPU:183, one launch (start us, length us, event | category | flops | bytes accessed | tf_op | source)
XLA Modules:
  0.0 104.6 jit_solution(11803958694634132818)
XLA Ops:
  0.0 102.2 %shooting.1 = f32[5,16,32,512]{3,2,1,0:T(8,128)S(1)} custom-call(f32[1,5,16,32,512]{4,3,2,1,0:T(8,128)} %a_ref.1, f32[1,16,32,512]{3,2,1,0:T(8,128)} %s_ref.1, f32[512,512]{1,0:T(8,128)} %w_ref.1, f32[5,5]{1,0:T(8,128)} %c_ref.1), custom_call_target="tpu_custom_call" | custom-call | tf_op jit(solution)/shard_map/shooting/pallas_call | solution.py:275
  102.3 2.4 %copy.6 = f32[1,5,16,32,512]{4,3,2,1,0:T(8,128)} copy(f32[1,5,16,32,512]{4,3,2,1,0:T(8,128)S(1)} %bitcast.1) | data formatting | bytes 10485760
where the time goes:
time: 106 us; the launch traced here: 105 us
  Pallas kernels  102 us (96%)
  local copies, waits for them, and re-layouts  2.36 us (2%)
    pallas_call x1, Pallas kernels, shards(): pl.pallas_call(kernel, out_shape=pltpu.VMEM((fields, cx, nt, nr), jnp.flo...  102 us
    unnamed x1, local copies, waits for them, and re-layouts  2.36 us

commit v1 on v0

--- a/solution.py
+++ b/solution.py
@@ -8,7 +8,7 @@
 from jax.sharding import PartitionSpec as P
 
 STEPS = 3
-FIRST = 2
+FIRST, SECOND = 2, 2
 MESH = pl.DeviceIdType.MESH
 
 
@@ -133,7 +133,7 @@
         planes[pl.ds(cx + STEPS, STEPS)] = jnp.zeros((STEPS, fields, nt, nr), jnp.float32)
 
     for step in range(STEPS):
-        for slot in range(3):
+        for slot in range(3 + STEPS):
             for f in range(fields):
                 mixd[step, slot, f, pl.ds(0, 8)] = jnp.zeros((8, nr), jnp.float32)
                 mixd[step, slot, f, pl.ds(8 + nt, 8)] = jnp.zeros((8, nr), jnp.float32)
@@ -160,23 +160,41 @@
     def arrival(i):
         plane_copy(0, i, i, (before, gx)).wait_recv()
 
-    @pl.when(jnp.logical_and(leaves, has_low))
-    def _():
-        for j in range(STEPS):
-            arrival(j)
-        pl.semaphore_signal(gsem, inc=1, device_id=(freed, low), device_id_type=MESH)
-
-    @pl.when(jnp.logical_and(leaves, has_high))
-    def _():
-        for j in range(STEPS):
-            arrival(STEPS + cx + j)
-        pl.semaphore_signal(gsem, inc=1, device_id=(freed, high), device_id_type=MESH)
-
-    @pl.when(leaves)
-    def _():
-        pl.semaphore_wait(gsem, lows + highs)
-        for j in range(FIRST, cx):
-            to_same(j).start()
+    def low_halo(first, stop, sem):
+        @pl.when(has_low)
+        def _():
+            for j in range(first, stop):
+                arrival(j)
+
+        @pl.when(jnp.logical_and(leaves, has_low))
+        def _():
+            pl.semaphore_signal(gsem.at[sem], inc=1, device_id=(freed, low), device_id_type=MESH)
+
+    def high_halo(first, stop, sem):
+        @pl.when(has_high)
+        def _():
+            for j in range(first, stop):
+                arrival(STEPS + cx + j)
+
+        @pl.when(jnp.logical_and(leaves, has_high))
+        def _():
+            pl.semaphore_signal(gsem.at[sem], inc=1, device_id=(freed, high), device_id_type=MESH)
+
+    def go(sem, count, start, stop):
+        @pl.when(jnp.logical_and(leaves, count > 0))
+        def _():
+            pl.semaphore_wait(gsem.at[sem], count)
+
+        @pl.when(leaves)
+        def _():
+            for j in range(start, stop):
+                to_same(j).start()
+
+    low_halo(0, STEPS - 1, 0)
+    high_halo(0, STEPS - 1, 0)
+    go(0, lows + highs, FIRST, FIRST + SECOND)
+    low_halo(STEPS - 1, STEPS, 1)
+    go(1, highs, FIRST + SECOND, cx)
 
     lane = lax.broadcasted_iota(jnp.int32, (half, nr), 1)
 
@@ -188,8 +206,16 @@
         xcat[rows, pl.ds(nr, nr)] = x_lo
         xcat[rows, pl.ds(2 * nr, nr)] = x_hi
 
+    ahead = STEPS + cx
+
+    def two_of(i):
+        return jnp.where(i < ahead, lax.rem(i, 2), i - ahead + 2)
+
+    def three_of(i):
+        return jnp.where(i < ahead, lax.rem(i, 3), i - ahead + 3)
+
     def filter_and_mix(step, i):
-        two, three = lax.rem(i, 2), lax.rem(i, 3)
+        two, three = two_of(i), three_of(i)
         filt[step, two] = jnp.dot(xcat[...], wcat[...], preferred_element_type=jnp.float32).reshape(fields, nt, nr)
         for t in range(nt // 8):
             rows = pl.ds(t * 8, 8)
@@ -201,8 +227,8 @@
                 mixd[step, three, f, pl.ds(8 + t * 8, 8)] = m
 
     def stencil(step, i, use):
-        two = lax.rem(i, 2)
-        mid, lo, hi = lax.rem(i, 3), lax.rem(i + 2, 3), lax.rem(i + 1, 3)
+        two = two_of(i)
+        mid, lo, hi = three_of(i), three_of(i - 1), three_of(i + 1)
         for h in range(2):
             s = sens[i - 1, pl.ds(h * half, half)]
             for f in range(fields):
@@ -215,23 +241,44 @@
                 total_ = total_ + left + right - 6.0 * m
                 use(f, h, filt[step, two, f, pl.ds(h * half, half)] + s * total_)
 
-    def arrive(i, carry):
-        slab = jnp.logical_and(i >= STEPS, i < STEPS + cx)
-        halo = jnp.logical_or(jnp.logical_and(i < STEPS, has_low), jnp.logical_and(i >= STEPS + cx, has_high))
-
-        @pl.when(jnp.logical_or(slab, jnp.logical_and(halo, jnp.logical_not(leaves))))
-        def _():
-            arrival(i)
-
+    def first_step(i):
         for h in range(2):
             for f in range(fields):
                 put(f, h, planes[i, f, pl.ds(h * half, half)])
         filter_and_mix(0, i)
 
-        @pl.when(i >= 2)
+    def early(i, carry):
+        first_step(i)
+        return carry
+
+    lax.fori_loop(ahead, total - 1, early, 0)
+
+    def last_halo():
+        @pl.when(has_high)
+        def _():
+            arrival(total - 1)
+
+        first_step(total - 1)
+        stencil(0, total - 2, put)
+        filter_and_mix(1, total - 2)
+
+    pl.when(jnp.logical_not(leaves))(last_halo)
+
+    def arrive(i, carry):
+        @pl.when(i < ahead)
+        def _():
+            @pl.when(i >= STEPS)
+            def _():
+                arrival(i)
+
+            first_step(i)
+
+        @pl.when(jnp.logical_and(i >= 2, i < total - 1))
         def _():
             stencil(0, i - 1, put)
             filter_and_mix(1, i - 1)
+
+        pl.when(jnp.logical_and(leaves, i == total - 1))(last_halo)
 
         @pl.when(i >= 4)
         def _():
@@ -289,12 +336,12 @@
             pltpu.VMEM((nr, nr), jnp.float32),
             pltpu.VMEM((3 * nr, nr), jnp.bfloat16),
             pltpu.VMEM((fields * nt, 3 * nr), jnp.bfloat16),
-            pltpu.VMEM((STEPS, 2, fields, nt, nr), jnp.float32),
-            pltpu.VMEM((STEPS, 3, fields, nt + 16, nr), jnp.float32),
+            pltpu.VMEM((STEPS, 2 + STEPS, fields, nt, nr), jnp.float32),
+            pltpu.VMEM((STEPS, 3 + STEPS, fields, nt + 16, nr), jnp.float32),
             pltpu.SemaphoreType.DMA((total + 2,)),
             pltpu.SemaphoreType.DMA((total + 2,)),
             pltpu.SemaphoreType.DMA((cx + 2,)),
-            pltpu.SemaphoreType.REGULAR,
+            pltpu.SemaphoreType.REGULAR((2,)),
         ],
         compiler_params=pltpu.CompilerParams(collective_id=0, has_side_effects=True, vmem_limit_bytes=61_400_000),
         name="shooting",

time: 106 us -> 103 us (0.972)
  Pallas kernels: 102 us -> 100 us
    pallas_call x1, Pallas kernels: 102 us -> 100 us  [shards(): pl.pallas_call(kernel, out_shape=pltpu.VMEM((fields, cx, nt, nr), jnp.flo...]
where the time goes in v1:
time: 103 us; the launch traced here: 102 us
  Pallas kernels  100 us (97%)
  local copies, waits for them, and re-layouts  2.36 us (2%)
    pallas_call x1, Pallas kernels, shards(): pl.pallas_call(kernel, out_shape=pltpu.VMEM((fields, cx, nt, nr), jnp.flo...  100 us
    unnamed x1, local copies, waits for them, and re-layouts  2.36 us

profile of v1, /device:TPU:183, one launch (start us, length us, event | category | flops | bytes accessed | tf_op | source)
XLA Modules:
  0.0 102.5 jit_solution(13313840309157672198)
XLA Ops:
  0.0 100.1 %shooting.1 = f32[5,16,32,512]{3,2,1,0:T(8,128)S(1)} custom-call(f32[1,5,16,32,512]{4,3,2,1,0:T(8,128)} %a_ref.1, f32[1,16,32,512]{3,2,1,0:T(8,128)} %s_ref.1, f32[512,512]{1,0:T(8,128)} %w_ref.1, f32[5,5]{1,0:T(8,128)} %c_ref.1), custom_call_target="tpu_custom_call" | custom-call | tf_op jit(solution)/shard_map/shooting/pallas_call | solution.py:322
  100.1 2.4 %copy.6 = f32[1,5,16,32,512]{4,3,2,1,0:T(8,128)} copy(f32[1,5,16,32,512]{4,3,2,1,0:T(8,128)S(1)} %bitcast.1) | data formatting | bytes 10485760
